TPU v7x, 32 devices: a whole 2x2x4 slice. The times are simulated.
32 devices in a mesh: ctx: 8 (over z, x), tp: 4 (over y, core).
Axes of the slice: x: 2, y: 2, z: 4, core: 2. Of those that a mesh axis runs over, the one named last changes fastest.
Arguments:
- q_raw: bfloat16 [2048, 4096], P('ctx', 'tp'), may hold values from -36 to 36
- k_raw: bfloat16 [2048, 2048], P('ctx', 'tp'), may hold values from -36 to 36
- v_cur: bfloat16 [2048, 2048], P('ctx', 'tp'), may hold values from -6 to 6
- d_out: bfloat16 [2048, 4096], P('ctx', 'tp'), may hold values from -6 to 6
- q_gain: float32 [128], replicated, may hold values from 0.25 to 1.75
- k_gain: float32 [128], replicated, may hold values from 0.25 to 1.75
Outputs:
- dq_raw: bfloat16 [2048, 4096], P('ctx', 'tp')
- dk_raw: bfloat16 [2048, 2048], P('ctx', 'tp')
- dv: bfloat16 [2048, 2048], P('ctx', 'tp')
- q_gain_grad: float32 [128], replicated
- k_gain_grad: float32 [128], replicated
All inputs are finite; a program needn't handle non-finite values.
Results may differ from a plain program's by a relative error of at most 0.0077.
Values may be sent and summed in bfloat16 or wider, within the bound.
A program may use at most 64 MiB of HBM per device.

v0:
```python
import jax
import jax.numpy as jnp
from jax import lax
from jax.sharding import PartitionSpec as P

Q_HEADS = 32
KV_HEADS = 16
HEAD_DIM = 128
WINDOW = 1024
score_scale = 168.0 ** (-0.5)
epsilon = 1e-06


def shifted(value, axis, by):
    devices = lax.axis_size(axis)
    pairs = [(i, i + by) for i in range(devices) if 0 <= i + by < devices]
    return lax.ppermute(value, axis, pairs)


def normalize(raw32, gain):
    vectors = raw32.reshape(raw32.shape[0], -1, HEAD_DIM)
    inverse = lax.rsqrt(jnp.mean(vectors * vectors, axis=-1, keepdims=True) + epsilon)
    return vectors * inverse * gain


def per_device(q_raw, k_raw, v_cur, d_out, q_gain, k_gain):
    row_count = q_raw.shape[0]
    hop_count = WINDOW // row_count
    q_normed, pull_query = jax.vjp(normalize, q_raw.astype(jnp.float32), q_gain)
    k_normed, pull_key = jax.vjp(normalize, k_raw.astype(jnp.float32), k_gain)
    q_low = q_normed.astype(jnp.bfloat16)
    k_low = k_normed.astype(jnp.bfloat16)
    local_kv = k_low.shape[1]
    local_q = q_low.shape[1]
    group = local_q // local_kv
    value_low = v_cur.reshape(row_count, local_kv, HEAD_DIM)
    grad_out = d_out.reshape(row_count, local_q, HEAD_DIM)
    earlier = []
    for distance in range(1, hop_count + 1):
        earlier.append(shifted((k_low, value_low), "ctx", distance))
    band_keys = jnp.concatenate(
        [earlier[d][0] for d in reversed(range(hop_count))] + [k_low], axis=0
    )
    band_values = jnp.concatenate(
        [earlier[d][1] for d in reversed(range(hop_count))] + [value_low], axis=0
    )
    band_width = (hop_count + 1) * row_count
    device_index = lax.axis_index("ctx")
    row_ids = lax.broadcasted_iota(jnp.int32, (row_count, band_width), 0)
    col_ids = lax.broadcasted_iota(jnp.int32, (row_count, band_width), 1)
    distance_ids = row_ids + hop_count * row_count - col_ids
    band_start = (device_index - hop_count) * row_count
    visible = (distance_ids >= 0) & (distance_ids < WINDOW) & (band_start + col_ids >= 0)
    dq_parts = []
    dk_parts = []
    dv_parts = []
    for kv_head in range(local_kv):
        queries = q_low[:, kv_head * group : (kv_head + 1) * group]
        grads = grad_out[:, kv_head * group : (kv_head + 1) * group]
        head_keys = band_keys[:, kv_head]
        head_values = band_values[:, kv_head]
        scores = (
            jnp.einsum("tgd,cd->gtc", queries, head_keys, preferred_element_type=jnp.float32)
            * score_scale
        )
        exp_scores = jnp.where(visible, jnp.exp(scores), 0.0)
        probs = exp_scores / jnp.sum(exp_scores, axis=-1, keepdims=True)
        dprobs = jnp.einsum("tgd,cd->gtc", grads, head_values, preferred_element_type=jnp.float32)
        row_delta = jnp.sum(probs * dprobs, axis=-1, keepdims=True)
        dscores = (probs * (dprobs - row_delta) * score_scale).astype(jnp.bfloat16)
        probs_low = probs.astype(jnp.bfloat16)
        dq_parts.append(
            jnp.einsum("gtc,cd->tgd", dscores, head_keys, preferred_element_type=jnp.float32)
        )
        dk_parts.append(
            jnp.einsum("gtc,tgd->cd", dscores, queries, preferred_element_type=jnp.float32).astype(
                jnp.bfloat16
            )
        )
        dv_parts.append(
            jnp.einsum("gtc,tgd->cd", probs_low, grads, preferred_element_type=jnp.float32).astype(
                jnp.bfloat16
            )
        )
    query_grad = jnp.concatenate(dq_parts, axis=1)
    key_blocks = jnp.stack(dk_parts, axis=1).reshape(hop_count + 1, row_count, local_kv, HEAD_DIM)
    value_blocks = jnp.stack(dv_parts, axis=1).reshape(hop_count + 1, row_count, local_kv, HEAD_DIM)
    key_grad = key_blocks[hop_count].astype(jnp.float32)
    value_grad = value_blocks[hop_count].astype(jnp.float32)
    for distance in range(1, hop_count + 1):
        got_key, got_value = shifted(
            (key_blocks[hop_count - distance], value_blocks[hop_count - distance]), "ctx", -distance
        )
        key_grad = key_grad + got_key.astype(jnp.float32)
        value_grad = value_grad + got_value.astype(jnp.float32)
    dq_raw32, q_gain_part = pull_query(query_grad)
    dk_raw32, k_gain_part = pull_key(key_grad)
    gain_totals = lax.psum((q_gain_part, k_gain_part), ("ctx", "tp"))
    token_total = row_count * lax.axis_size("ctx")
    q_gain_grad = gain_totals[0] / jnp.sqrt(jnp.float32(token_total * Q_HEADS))
    k_gain_grad = gain_totals[1] / jnp.sqrt(jnp.float32(token_total * KV_HEADS))
    dq_raw = dq_raw32.astype(jnp.bfloat16)
    dk_raw = dk_raw32.astype(jnp.bfloat16)
    dv = value_grad.reshape(row_count, -1).astype(jnp.bfloat16)
    return (dq_raw, dk_raw, dv, q_gain_grad, k_gain_grad)


def solution(mesh):
    return jax.shard_map(
        per_device,
        mesh=mesh,
        in_specs=(P("ctx", "tp"), P("ctx", "tp"), P("ctx", "tp"), P("ctx", "tp"), P(), P()),
        out_specs=(P("ctx", "tp"), P("ctx", "tp"), P("ctx", "tp"), P(), P()),
        check_vma=False,
    )
```

profile of v0, /device:TPU:0, one launch (start us, length us, event | category | flops | bytes accessed | tf_op | source)
XLA Modules:
  0.0 263.9 jit_solution(4225913662095262754)
XLA Ops:
  2.0 5.5 %collective-permute-start.7 = (bf16[256,4,128]{2,0,1:T(8,128)(2,1)S(1)}, bf16[256,4,128]{2,0,1:T(8,128)(2,1)}, u32[]{:S(2)}, u32[]{:S(2)}) collective-permute-start(bf16[256,4,128]{2,0,1:T(8,128)(2,1)S(1)} %copy.106), channel_id=1, source_target_pairs={{0,4},{4,8},{8,12},{12,16},{16,20},{20,24},{24,28},{1,5},{5,9},{9,... | collective-permute-start | bytes 786440 | tf_op jit(solution)/shard_map/ppermute | solution.py:17
  7.5 3.5 %collective-permute-start.6 = (bf16[256,4,128]{2,0,1:T(8,128)(2,1)S(1)}, bf16[256,4,128]{2,0,1:T(8,128)(2,1)}, u32[]{:S(2)}, u32[]{:S(2)}) collective-permute-start(bf16[256,4,128]{2,0,1:T(8,128)(2,1)S(1)} %copy.106), channel_id=1, source_target_pairs={{0,8},{4,12},{8,16},{12,20},{16,24},{20,28},{1,9},{5,13},{9,17},{1... | collective-permute-start | bytes 786440 | tf_op jit(solution)/shard_map/ppermute | solution.py:17
  13.3 3.6 %collective-permute-start.2 = (bf16[256,4,128]{2,0,1:T(8,128)(2,1)}, bf16[256,4,128]{2,0,1:T(8,128)(2,1)}, u32[]{:S(2)}, u32[]{:S(2)}) collective-permute-start(bf16[256,4,128]{2,0,1:T(8,128)(2,1)} %multiply_convert_fusion.1), channel_id=1, source_target_pairs={{0,8},{4,12},{8,16},{12,20},{16,24},{20,28},{1,9},{5,13},{9,17},{1... | collective-permute-start | bytes 786440 | tf_op jit(solution)/shard_map/ppermute | solution.py:17
  16.9 2.9 %collective-permute-start.1 = (bf16[256,4,128]{2,0,1:T(8,128)(2,1)}, bf16[256,4,128]{2,0,1:T(8,128)(2,1)}, u32[]{:S(2)}, u32[]{:S(2)}) collective-permute-start(bf16[256,4,128]{2,0,1:T(8,128)(2,1)} %multiply_convert_fusion.1), channel_id=1, source_target_pairs={{0,12},{4,16},{8,20},{12,24},{16,28},{1,13},{5,17},{9,21},{13,25},... | collective-permute-start | bytes 786440 | tf_op jit(solution)/shard_map/ppermute | solution.py:17
  19.8 2.0 collective-permute-start
  24.8 8.0 %collective-permute-done = bf16[256,4,128]{2,0,1:T(8,128)(2,1)} collective-permute-done((bf16[256,4,128]{2,0,1:T(8,128)(2,1)}, bf16[256,4,128]{2,0,1:T(8,128)(2,1)}, u32[]{:S(2)}, u32[]{:S(2)}) %collective-permute-start) | collective-permute-done | bytes 262176 | tf_op jit(solution)/shard_map/ppermute | solution.py:17
  32.8 5.7 %collective-permute-start.3 = (bf16[256,4,128]{2,0,1:T(8,128)(2,1)}, bf16[256,4,128]{2,0,1:T(8,128)(2,1)S(1)}, u32[]{:S(2)}, u32[]{:S(2)}) collective-permute-start(bf16[256,4,128]{2,0,1:T(8,128)(2,1)} %multiply_convert_fusion.1), channel_id=1, source_target_pairs={{0,4},{4,8},{8,12},{12,16},{16,20},{20,24},{24,28},{1,5},{5,9},{9,... | collective-permute-start | bytes 786440 | tf_op jit(solution)/shard_map/ppermute | solution.py:17
  38.5 1.7 constant_dynamic-update-slice_fusion.4
  40.2 16.8 %collective-permute-start.5 = (bf16[256,4,128]{2,0,1:T(8,128)(2,1)S(1)}, bf16[256,4,128]{2,0,1:T(8,128)(2,1)}, u32[]{:S(2)}, u32[]{:S(2)}) collective-permute-start(bf16[256,4,128]{2,0,1:T(8,128)(2,1)S(1)} %copy.106), channel_id=1, source_target_pairs={{0,12},{4,16},{8,20},{12,24},{16,28},{1,13},{5,17},{9,21},{13,25},... | collective-permute-start | bytes 786440 | tf_op jit(solution)/shard_map/ppermute | solution.py:17
  56.9 1.7 constant_dynamic-update-slice_fusion.3
  58.6 14.0 %collective-permute-start.4 = (bf16[256,4,128]{2,0,1:T(8,128)(2,1)S(1)}, bf16[256,4,128]{2,0,1:T(8,128)(2,1)}, u32[]{:S(2)}, u32[]{:S(2)}) collective-permute-start(bf16[256,4,128]{2,0,1:T(8,128)(2,1)S(1)} %copy.106), channel_id=1, source_target_pairs={{0,16},{4,20},{8,24},{12,28},{1,17},{5,21},{9,25},{13,29},{2,18},{... | collective-permute-start | bytes 786440 | tf_op jit(solution)/shard_map/ppermute | solution.py:17
  72.7 1.7 constant_dynamic-update-slice_fusion.2
  76.1 3.5 %fusion.77 = f32[2,256,1280]{1,2,0:T(8,128)} fusion(pred[256,1280]{0,1:T(8,128)(4,1)} %fusion.95, bf16[1280,4,128]{2,0,1:T(8,128)(2,1)} %constant_dynamic-update-slice_fusion, bf16[256,8,128]{2,0,1:T(8,128)(2,1)S(1)} %copy-done.7), kind=kOutput, calls=%fused_computation.86 | convolution fusion | flops 169740032 | bytes 3407872 | tf_op jit(solution)/shard_map/div | solution.py:67
  79.6 3.5 %fusion.79 = f32[2,256,1280]{1,2,0:T(8,128)} fusion(pred[256,1280]{0,1:T(8,128)(4,1)} %fusion.95, bf16[1280,4,128]{2,0,1:T(8,128)(2,1)} %constant_dynamic-update-slice_fusion, bf16[256,8,128]{2,0,1:T(8,128)(2,1)S(1)} %copy-done.7), kind=kOutput, calls=%fused_computation.88 | convolution fusion | flops 169740032 | bytes 3407872 | tf_op jit(solution)/shard_map/div | solution.py:67
  83.0 3.5 %fusion.81 = f32[2,256,1280]{1,2,0:T(8,128)} fusion(pred[256,1280]{0,1:T(8,128)(4,1)} %fusion.95, bf16[1280,4,128]{2,0,1:T(8,128)(2,1)} %constant_dynamic-update-slice_fusion, bf16[256,8,128]{2,0,1:T(8,128)(2,1)S(1)} %copy-done.7), kind=kOutput, calls=%fused_computation.90 | convolution fusion | flops 169740032 | bytes 3407872 | tf_op jit(solution)/shard_map/div | solution.py:67
  86.5 3.5 %fusion.91 = f32[2,256,1280]{1,2,0:T(8,128)} fusion(pred[256,1280]{0,1:T(8,128)(4,1)} %fusion.95, bf16[1280,4,128]{2,0,1:T(8,128)(2,1)} %constant_dynamic-update-slice_fusion, bf16[256,8,128]{2,0,1:T(8,128)(2,1)S(1)} %copy-done.7), kind=kOutput, calls=%fused_computation.100 | convolution fusion | flops 169740032 | bytes 3407872 | tf_op jit(solution)/shard_map/div | solution.py:67
  95.5 2.0 convolution_bitcast_fusion
  97.5 5.8 %fusion.96 = f32[256,2,128]{2,0,1:T(8,128)} fusion(f32[2,256,1280]{1,2,0:T(8,128)} %fusion.77, f32[2,256,1280]{1,2,0:T(8,128)} %convolution_bitcast_fusion, bf16[1280,4,128]{2,0,1:T(8,128)(2,1)} %constant_dynamic-update-slice_fusion), kind=kOutput, calls=%fused_computation.106 | convolution fusion | flops 171050752 | bytes 11075584 | tf_op jit(solution)/shard_map/gtc,cd->tgd/dot_general | solution.py:73
  103.3 5.6 %fusion.48 = bf16[1280,1,128]{2,0,1:T(8,128)(2,1)} fusion(f32[2,256,1280]{1,2,0:T(8,128)} %fusion.77, f32[2,256,1280]{1,2,0:T(8,128)} %convolution_bitcast_fusion, bf16[256,8,128]{2,0,1:T(8,128)(2,1)S(1)} %copy-done.7), kind=kOutput, calls=%fused_computation.68 | convolution fusion | flops 171214592 | bytes 10944512 | tf_op jit(solution)/shard_map/gtc,tgd->cd/dot_general | solution.py:76
  108.9 3.2 %convolution_bitcast_fusion.1 = f32[2,256,1280]{1,2,0:T(8,128)} fusion(bf16[1280,4,128]{2,0,1:T(8,128)(2,1)} %copy-done.4, bf16[256,8,128]{0,2,1:T(8,128)(2,1)S(1)} %bitcast.191), kind=kOutput, calls=%fused_computation.21 | convolution fusion | flops 167772160 | bytes 3080192 | tf_op jit(solution)/shard_map/tgd,cd->gtc/dot_general | solution.py:68
  113.3 5.8 %fusion.99 = f32[256,2,128]{2,0,1:T(8,128)} fusion(f32[2,256,1280]{1,2,0:T(8,128)} %fusion.79, f32[2,256,1280]{1,2,0:T(8,128)} %convolution_bitcast_fusion.1, bf16[1280,4,128]{2,0,1:T(8,128)(2,1)} %constant_dynamic-update-slice_fusion), kind=kOutput, calls=%fused_computation.107 | convolution fusion | flops 171050752 | bytes 11075584 | tf_op jit(solution)/shard_map/gtc,cd->tgd/dot_general | solution.py:73
  119.1 5.6 %fusion.49 = bf16[1280,1,128]{2,0,1:T(8,128)(2,1)} fusion(f32[2,256,1280]{1,2,0:T(8,128)} %fusion.79, f32[2,256,1280]{1,2,0:T(8,128)} %convolution_bitcast_fusion.1, bf16[256,8,128]{2,0,1:T(8,128)(2,1)S(1)} %copy-done.7), kind=kOutput, calls=%fused_computation.69 | convolution fusion | flops 171214592 | bytes 10944512 | tf_op jit(solution)/shard_map/gtc,tgd->cd/dot_general | solution.py:76
  124.7 3.1 %convolution_bitcast_fusion.2 = f32[2,256,1280]{1,2,0:T(8,128)} fusion(bf16[1280,4,128]{2,0,1:T(8,128)(2,1)} %copy-done.4, bf16[256,8,128]{0,2,1:T(8,128)(2,1)S(1)} %bitcast.193), kind=kOutput, calls=%fused_computation.22 | convolution fusion | flops 167772160 | bytes 3080192 | tf_op jit(solution)/shard_map/tgd,cd->gtc/dot_general | solution.py:68
  129.1 5.8 %fusion.102 = f32[256,2,128]{2,0,1:T(8,128)} fusion(f32[2,256,1280]{1,2,0:T(8,128)} %fusion.81, f32[2,256,1280]{1,2,0:T(8,128)} %convolution_bitcast_fusion.2, bf16[1280,4,128]{2,0,1:T(8,128)(2,1)} %constant_dynamic-update-slice_fusion), kind=kOutput, calls=%fused_computation.108 | convolution fusion | flops 171050752 | bytes 11075584 | tf_op jit(solution)/shard_map/gtc,cd->tgd/dot_general | solution.py:73
  134.9 5.6 %fusion.50 = bf16[1280,1,128]{2,0,1:T(8,128)(2,1)} fusion(f32[2,256,1280]{1,2,0:T(8,128)} %fusion.81, f32[2,256,1280]{1,2,0:T(8,128)} %convolution_bitcast_fusion.2, bf16[256,8,128]{2,0,1:T(8,128)(2,1)S(1)} %copy-done.7), kind=kOutput, calls=%fused_computation.70 | convolution fusion | flops 171214592 | bytes 10944512 | tf_op jit(solution)/shard_map/gtc,tgd->cd/dot_general | solution.py:76
  140.5 3.1 %convolution_bitcast_fusion.3 = f32[2,256,1280]{1,2,0:T(8,128)} fusion(bf16[1280,4,128]{2,0,1:T(8,128)(2,1)} %copy-done.4, bf16[256,8,128]{0,2,1:T(8,128)(2,1)S(1)} %bitcast.195), kind=kOutput, calls=%fused_computation.23 | convolution fusion | flops 167772160 | bytes 3080192 | tf_op jit(solution)/shard_map/tgd,cd->gtc/dot_general | solution.py:68
  144.9 6.0 %fusion.105 = f32[256,2,128]{2,0,1:T(8,128)} fusion(f32[2,256,1280]{1,2,0:T(8,128)} %fusion.91, f32[2,256,1280]{1,2,0:T(8,128)} %convolution_bitcast_fusion.3, bf16[1280,4,128]{2,0,1:T(8,128)(2,1)} %constant_dynamic-update-slice_fusion), kind=kOutput, calls=%fused_computation.109 | convolution fusion | flops 171050752 | bytes 11075584 | tf_op jit(solution)/shard_map/gtc,cd->tgd/dot_general | solution.py:73
  151.0 5.6 %fusion.51 = bf16[1280,1,128]{2,0,1:T(8,128)(2,1)} fusion(f32[2,256,1280]{1,2,0:T(8,128)} %fusion.91, f32[2,256,1280]{1,2,0:T(8,128)} %convolution_bitcast_fusion.3, bf16[256,8,128]{2,0,1:T(8,128)(2,1)S(1)} %copy-done.7), kind=kOutput, calls=%fused_computation.71 | convolution fusion | flops 171214592 | bytes 10944512 | tf_op jit(solution)/shard_map/gtc,tgd->cd/dot_general | solution.py:76
  168.3 2.0 copy.154
  175.4 12.9 %collective-permute-done.15 = bf16[256,4,128]{0,2,1:T(8,128)(2,1)} collective-permute-done((bf16[256,4,128]{0,2,1:T(8,128)(2,1)}, bf16[256,4,128]{0,2,1:T(8,128)(2,1)}, u32[]{:S(2)}, u32[]{:S(2)}) %collective-permute-start.15) | collective-permute-done | bytes 262176 | tf_op jit(solution)/shard_map/ppermute | solution.py:17
  193.1 23.3 %collective-permute-done.11 = bf16[256,4,128]{2,0,1:T(8,128)(2,1)} collective-permute-done((bf16[256,4,128]{2,0,1:T(8,128)(2,1)}, bf16[256,4,128]{2,0,1:T(8,128)(2,1)}, u32[]{:S(2)}, u32[]{:S(2)}) %collective-permute-start.11) | collective-permute-done | bytes 262176 | tf_op jit(solution)/shard_map/ppermute | solution.py:17
  219.3 44.1 %all-reduce = (f32[128]{0:T(128)S(1)}, f32[128]{0:T(128)S(1)}) all-reduce(f32[128]{0:T(128)S(1)} %bitcast_reduce_fusion, f32[128]{0:T(128)S(1)} %get-tuple-element.20), channel_id=1, replica_groups=mesh['ctx'=8,'tp'=4] {'ctx','tp'}, use_global_device_ids=true, to_apply=%region_14.15 | all-reduce | flops 256 | bytes 2048 | tf_op jit(solution)/shard_map/psum | solution.py:98
  (94 shorter events, 42.4 us)
Async XLA Ops:
  0.6 11.7 %copy-start.12 = (f32[128]{0:T(128)S(1)}, f32[128]{0:T(128)}, u32[]{:S(2)}) copy-start(f32[128]{0:T(128)} %param.11) | copy-start | bytes 1540
  0.6 21.1 %copy-start.5 = (bf16[256,1024]{1,0:T(8,128)(2,1)S(1)}, bf16[256,1024]{1,0:T(8,128)(2,1)}, u32[]{:S(2)}) copy-start(bf16[256,1024]{1,0:T(8,128)(2,1)} %param.6) | copy-start | bytes 1572868
  2.0 91.1 %collective-permute-start.7 = (bf16[256,4,128]{2,0,1:T(8,128)(2,1)S(1)}, bf16[256,4,128]{2,0,1:T(8,128)(2,1)}, u32[]{:S(2)}, u32[]{:S(2)}) collective-permute-start(bf16[256,4,128]{2,0,1:T(8,128)(2,1)S(1)} %copy.106), channel_id=1, source_target_pairs={{0,4},{4,8},{8,12},{12,16},{16,20},{20,24},{24,28},{1,5},{5,9},{9,... | collective-permute-start | bytes 786440 | tf_op jit(solution)/shard_map/ppermute | solution.py:17
  7.5 84.6 %collective-permute-start.6 = (bf16[256,4,128]{2,0,1:T(8,128)(2,1)S(1)}, bf16[256,4,128]{2,0,1:T(8,128)(2,1)}, u32[]{:S(2)}, u32[]{:S(2)}) collective-permute-start(bf16[256,4,128]{2,0,1:T(8,128)(2,1)S(1)} %copy.106), channel_id=1, source_target_pairs={{0,8},{4,12},{8,16},{12,20},{16,24},{20,28},{1,9},{5,13},{9,17},{1... | collective-permute-start | bytes 786440 | tf_op jit(solution)/shard_map/ppermute | solution.py:17
  12.1 11.3 %copy-start.13 = (f32[128]{0:T(128)S(1)}, f32[128]{0:T(128)}, u32[]{:S(2)}) copy-start(f32[128]{0:T(128)} %param.10) | copy-start | bytes 1540
  13.3 11.3 %copy-start.6 = (bf16[256,1024]{1,0:T(8,128)(2,1)S(1)}, bf16[256,1024]{1,0:T(8,128)(2,1)}, u32[]{:S(2)}) copy-start(bf16[256,1024]{1,0:T(8,128)(2,1)} %param.9) | copy-start | bytes 1572868
  13.3 45.4 %collective-permute-start.2 = (bf16[256,4,128]{2,0,1:T(8,128)(2,1)}, bf16[256,4,128]{2,0,1:T(8,128)(2,1)}, u32[]{:S(2)}, u32[]{:S(2)}) collective-permute-start(bf16[256,4,128]{2,0,1:T(8,128)(2,1)} %multiply_convert_fusion.1), channel_id=1, source_target_pairs={{0,8},{4,12},{8,16},{12,20},{16,24},{20,28},{1,9},{5,13},{9,17},{1... | collective-permute-start | bytes 786440 | tf_op jit(solution)/shard_map/ppermute | solution.py:17
  16.9 23.3 %collective-permute-start.1 = (bf16[256,4,128]{2,0,1:T(8,128)(2,1)}, bf16[256,4,128]{2,0,1:T(8,128)(2,1)}, u32[]{:S(2)}, u32[]{:S(2)}) collective-permute-start(bf16[256,4,128]{2,0,1:T(8,128)(2,1)} %multiply_convert_fusion.1), channel_id=1, source_target_pairs={{0,12},{4,16},{8,20},{12,24},{16,28},{1,13},{5,17},{9,21},{13,25},... | collective-permute-start | bytes 786440 | tf_op jit(solution)/shard_map/ppermute | solution.py:17
  19.8 13.0 %collective-permute-start = (bf16[256,4,128]{2,0,1:T(8,128)(2,1)}, bf16[256,4,128]{2,0,1:T(8,128)(2,1)}, u32[]{:S(2)}, u32[]{:S(2)}) collective-permute-start(bf16[256,4,128]{2,0,1:T(8,128)(2,1)} %multiply_convert_fusion.1), channel_id=1, source_target_pairs={{0,16},{4,20},{8,24},{12,28},{1,17},{5,21},{9,25},{13,29},{2,18},{... | collective-permute-start | bytes 786440 | tf_op jit(solution)/shard_map/ppermute | solution.py:17
  24.8 51.2 %copy-start.7 = (bf16[256,8,128]{2,0,1:T(8,128)(2,1)S(1)}, bf16[256,8,128]{2,0,1:T(8,128)(2,1)}, u32[]{:S(2)}) copy-start(bf16[256,8,128]{2,0,1:T(8,128)(2,1)} %multiply_convert_fusion) | copy-start | bytes 1572868
  32.8 41.6 %collective-permute-start.3 = (bf16[256,4,128]{2,0,1:T(8,128)(2,1)}, bf16[256,4,128]{2,0,1:T(8,128)(2,1)S(1)}, u32[]{:S(2)}, u32[]{:S(2)}) collective-permute-start(bf16[256,4,128]{2,0,1:T(8,128)(2,1)} %multiply_convert_fusion.1), channel_id=1, source_target_pairs={{0,4},{4,8},{8,12},{12,16},{16,20},{20,24},{24,28},{1,5},{5,9},{9,... | collective-permute-start | bytes 786440 | tf_op jit(solution)/shard_map/ppermute | solution.py:17
  40.2 51.0 %collective-permute-start.5 = (bf16[256,4,128]{2,0,1:T(8,128)(2,1)S(1)}, bf16[256,4,128]{2,0,1:T(8,128)(2,1)}, u32[]{:S(2)}, u32[]{:S(2)}) collective-permute-start(bf16[256,4,128]{2,0,1:T(8,128)(2,1)S(1)} %copy.106), channel_id=1, source_target_pairs={{0,12},{4,16},{8,20},{12,24},{16,28},{1,13},{5,17},{9,21},{13,25},... | collective-permute-start | bytes 786440 | tf_op jit(solution)/shard_map/ppermute | solution.py:17
  58.6 31.4 %collective-permute-start.4 = (bf16[256,4,128]{2,0,1:T(8,128)(2,1)S(1)}, bf16[256,4,128]{2,0,1:T(8,128)(2,1)}, u32[]{:S(2)}, u32[]{:S(2)}) collective-permute-start(bf16[256,4,128]{2,0,1:T(8,128)(2,1)S(1)} %copy.106), channel_id=1, source_target_pairs={{0,16},{4,20},{8,24},{12,28},{1,17},{5,21},{9,25},{13,29},{2,18},{... | collective-permute-start | bytes 786440 | tf_op jit(solution)/shard_map/ppermute | solution.py:17
  90.0 4.2 %copy-start.3 = (f32[2,256,1280]{1,2,0:T(8,128)S(1)}, f32[2,256,1280]{1,2,0:T(8,128)}, u32[]{:S(2)}) copy-start(f32[2,256,1280]{1,2,0:T(8,128)} %fusion.77) | copy-start | bytes 7864324
  94.2 1.3 copy-start.4
  108.9 3.2 %copy-start.2 = (f32[2,256,1280]{1,2,0:T(8,128)S(1)}, f32[2,256,1280]{1,2,0:T(8,128)}, u32[]{:S(2)}) copy-start(f32[2,256,1280]{1,2,0:T(8,128)} %fusion.79) | copy-start | bytes 7864324
  124.7 3.1 %copy-start.1 = (f32[2,256,1280]{1,2,0:T(8,128)S(1)}, f32[2,256,1280]{1,2,0:T(8,128)}, u32[]{:S(2)}) copy-start(f32[2,256,1280]{1,2,0:T(8,128)} %fusion.81) | copy-start | bytes 7864324
  140.5 3.1 %copy-start = (f32[2,256,1280]{1,2,0:T(8,128)S(1)}, f32[2,256,1280]{1,2,0:T(8,128)}, u32[]{:S(2)}) copy-start(f32[2,256,1280]{1,2,0:T(8,128)} %fusion.91) | copy-start | bytes 7864324
  156.6 7.7 %copy-start.8 = (f32[256,2,128]{2,0,1:T(8,128)S(1)}, f32[256,2,128]{2,0,1:T(8,128)}, u32[]{:S(2)}) copy-start(f32[256,2,128]{2,0,1:T(8,128)} %fusion.96) | copy-start | bytes 786436
  156.6 7.7 %copy-start.9 = (f32[256,2,128]{2,0,1:T(8,128)S(1)}, f32[256,2,128]{2,0,1:T(8,128)}, u32[]{:S(2)}) copy-start(f32[256,2,128]{2,0,1:T(8,128)} %fusion.99) | copy-start | bytes 786436
  156.6 7.7 %copy-start.10 = (f32[256,2,128]{2,0,1:T(8,128)S(1)}, f32[256,2,128]{2,0,1:T(8,128)}, u32[]{:S(2)}) copy-start(f32[256,2,128]{2,0,1:T(8,128)} %fusion.102) | copy-start | bytes 786436
  156.6 7.7 %copy-start.11 = (f32[256,2,128]{2,0,1:T(8,128)S(1)}, f32[256,2,128]{2,0,1:T(8,128)}, u32[]{:S(2)}) copy-start(f32[256,2,128]{2,0,1:T(8,128)} %fusion.105) | copy-start | bytes 786436
  159.1 15.0 %collective-permute-start.12 = (bf16[256,4,128]{0,2,1:T(8,128)(2,1)}, bf16[256,4,128]{0,2,1:T(8,128)(2,1)}, u32[]{:S(2)}, u32[]{:S(2)}) collective-permute-start(bf16[256,4,128]{0,2,1:T(8,128)(2,1)} %get-tuple-element.27), channel_id=1, source_target_pairs={{4,0},{8,4},{12,8},{16,12},{20,16},{24,20},{28,24},{5,1},{9,5},{13... | collective-permute-start | bytes 786440 | tf_op jit(solution)/shard_map/ppermute | solution.py:17
  160.4 27.9 %collective-permute-start.15 = (bf16[256,4,128]{0,2,1:T(8,128)(2,1)}, bf16[256,4,128]{0,2,1:T(8,128)(2,1)}, u32[]{:S(2)}, u32[]{:S(2)}) collective-permute-start(bf16[256,4,128]{0,2,1:T(8,128)(2,1)} %get-tuple-element.28), channel_id=1, source_target_pairs={{16,0},{20,4},{24,8},{28,12},{17,1},{21,5},{25,9},{29,13},{18,2},{... | collective-permute-start | bytes 786440 | tf_op jit(solution)/shard_map/ppermute | solution.py:17
  161.7 27.9 %collective-permute-start.14 = (bf16[256,4,128]{0,2,1:T(8,128)(2,1)}, bf16[256,4,128]{0,2,1:T(8,128)(2,1)}, u32[]{:S(2)}, u32[]{:S(2)}) collective-permute-start(bf16[256,4,128]{0,2,1:T(8,128)(2,1)} %get-tuple-element.29), channel_id=1, source_target_pairs={{12,0},{16,4},{20,8},{24,12},{28,16},{13,1},{17,5},{21,9},{25,13},... | collective-permute-start | bytes 786440 | tf_op jit(solution)/shard_map/ppermute | solution.py:17
  163.0 27.9 %collective-permute-start.13 = (bf16[256,4,128]{0,2,1:T(8,128)(2,1)}, bf16[256,4,128]{0,2,1:T(8,128)(2,1)}, u32[]{:S(2)}, u32[]{:S(2)}) collective-permute-start(bf16[256,4,128]{0,2,1:T(8,128)(2,1)} %get-tuple-element.30), channel_id=1, source_target_pairs={{8,0},{12,4},{16,8},{20,12},{24,16},{28,20},{9,1},{13,5},{17,9},{2... | collective-permute-start | bytes 786440 | tf_op jit(solution)/shard_map/ppermute | solution.py:17
  172.8 20.3 %collective-permute-start.8 = (bf16[256,4,128]{2,0,1:T(8,128)(2,1)}, bf16[256,4,128]{2,0,1:T(8,128)(2,1)}, u32[]{:S(2)}, u32[]{:S(2)}) collective-permute-start(bf16[256,4,128]{2,0,1:T(8,128)(2,1)} %get-tuple-element.31), channel_id=1, source_target_pairs={{4,0},{8,4},{12,8},{16,12},{20,16},{24,20},{28,24},{5,1},{9,5},{13... | collective-permute-start | bytes 786440 | tf_op jit(solution)/shard_map/ppermute | solution.py:17
  174.1 42.2 %collective-permute-start.11 = (bf16[256,4,128]{2,0,1:T(8,128)(2,1)}, bf16[256,4,128]{2,0,1:T(8,128)(2,1)}, u32[]{:S(2)}, u32[]{:S(2)}) collective-permute-start(bf16[256,4,128]{2,0,1:T(8,128)(2,1)} %get-tuple-element.32), channel_id=1, source_target_pairs={{16,0},{20,4},{24,8},{28,12},{17,1},{21,5},{25,9},{29,13},{18,2},{... | collective-permute-start | bytes 786440 | tf_op jit(solution)/shard_map/ppermute | solution.py:17
  188.3 28.1 %collective-permute-start.10 = (bf16[256,4,128]{2,0,1:T(8,128)(2,1)}, bf16[256,4,128]{2,0,1:T(8,128)(2,1)}, u32[]{:S(2)}, u32[]{:S(2)}) collective-permute-start(bf16[256,4,128]{2,0,1:T(8,128)(2,1)} %get-tuple-element.33), channel_id=1, source_target_pairs={{12,0},{16,4},{20,8},{24,12},{28,16},{13,1},{17,5},{21,9},{25,13},... | collective-permute-start | bytes 786440 | tf_op jit(solution)/shard_map/ppermute | solution.py:17
  189.6 26.8 %collective-permute-start.9 = (bf16[256,4,128]{2,0,1:T(8,128)(2,1)}, bf16[256,4,128]{2,0,1:T(8,128)(2,1)}, u32[]{:S(2)}, u32[]{:S(2)}) collective-permute-start(bf16[256,4,128]{2,0,1:T(8,128)(2,1)} %get-tuple-element.34), channel_id=1, source_target_pairs={{8,0},{12,4},{16,8},{20,12},{24,16},{28,20},{9,1},{13,5},{17,9},{2... | collective-permute-start | bytes 786440 | tf_op jit(solution)/shard_map/ppermute | solution.py:17
where the time goes:
time: 265 us; the launch traced here: 264 us
  matrix products  76.3 us (29%)
  starting transfers between devices  64.3 us (24%)
  waiting for transfers between devices  44.1 us (17%)
  blocking collectives  44.1 us (17%)
  local copies, waits for them, and re-layouts  20.6 us (8%)
  other arithmetic  13.5 us (5%)
    ppermute x16, starting transfers between devices, shifted(): return lax.ppermute(value, axis, pairs)  64.3 us
    ppermute x16, waiting for transfers between devices, shifted(): return lax.ppermute(value, axis, pairs)  44.1 us
    psum x1, blocking collectives, per_device(): gain_totals = lax.psum((q_gain_part, k_gain_part), ('ctx', 'tp'))  44.1 us
    dot_general x4, matrix products, per_device(): jnp.einsum('gtc,cd->tgd', dscores, head_keys, preferred_element_type=jnp....  23.4 us
    dot_general x4, matrix products, per_device(): jnp.einsum('gtc,tgd->cd', dscores, queries, preferred_element_type=jnp.fl...  22.4 us
    unnamed x43, local copies, waits for them, and re-layouts  16.3 us
    div x4, matrix products, per_device(): probs = exp_scores / jnp.sum(exp_scores, axis=-1, keepdims=True)  13.9 us
    dot_general x4, matrix products, per_device(): jnp.einsum('tgd,cd->gtc', grads, head_values, preferred_element_type=jnp....  11.4 us
  transfers between devices with their start and end apart: 16, of which 3 were waited for; matrix products, arithmetic and copies ran while one was open for 15% of the time, Pallas kernels for 0%

commit v1 on v0

--- a/solution.py
+++ b/solution.py
@@ -95,7 +95,8 @@
         value_grad = value_grad + got_value.astype(jnp.float32)
     dq_raw32, q_gain_part = pull_query(query_grad)
     dk_raw32, k_gain_part = pull_key(key_grad)
-    gain_totals = lax.psum((q_gain_part, k_gain_part), ("ctx", "tp"))
+    half = lax.psum((q_gain_part, k_gain_part), "tp")
+    gain_totals = lax.psum(half, "ctx")
     token_total = row_count * lax.axis_size("ctx")
     q_gain_grad = gain_totals[0] / jnp.sqrt(jnp.float32(token_total * Q_HEADS))
     k_gain_grad = gain_totals[1] / jnp.sqrt(jnp.float32(token_total * KV_HEADS))

time: 265 us -> 248 us (0.936)
  blocking collectives: 44.1 us -> 27.2 us
    psum x1 -> x2, blocking collectives: 44.1 us -> 27.2 us  [the longest x1 21.6 us: per_device(): gain_totals = lax.psum(half, 'ctx')]
  transfers between devices with their start and end apart: 16 -> 16, of which waited for: 3 -> 3; matrix products, arithmetic and copies ran while one was open for 15% -> 16% of each run, Pallas kernels for 0% -> 0%
where the time goes in v1:
time: 248 us; the launch traced here: 247 us
  matrix products  76.3 us (31%)
  starting transfers between devices  64.3 us (26%)
  waiting for transfers between devices  44.1 us (18%)
  blocking collectives  27.2 us (11%)
  local copies, waits for them, and re-layouts  20.6 us (8%)
  other arithmetic  13.5 us (5%)
    ppermute x16, starting transfers between devices, shifted(): return lax.ppermute(value, axis, pairs)  64.3 us
    ppermute x16, waiting for transfers between devices, shifted(): return lax.ppermute(value, axis, pairs)  44.1 us
    dot_general x4, matrix products, per_device(): jnp.einsum('gtc,cd->tgd', dscores, head_keys, preferred_element_type=jnp....  23.4 us
    dot_general x4, matrix products, per_device(): jnp.einsum('gtc,tgd->cd', dscores, queries, preferred_element_type=jnp.fl...  22.4 us
    psum x1, blocking collectives, per_device(): gain_totals = lax.psum(half, 'ctx')  21.6 us
    unnamed x43, local copies, waits for them, and re-layouts  16.3 us
    div x4, matrix products, per_device(): probs = exp_scores / jnp.sum(exp_scores, axis=-1, keepdims=True)  13.9 us
    dot_general x4, matrix products, per_device(): jnp.einsum('tgd,cd->gtc', grads, head_values, preferred_element_type=jnp....  11.4 us
  transfers between devices with their start and end apart: 16, of which 3 were waited for; matrix products, arithmetic and copies ran while one was open for 16% of the time, Pallas kernels for 0%

profile of v1, /device:TPU:0, one launch (start us, length us, event | category | flops | bytes accessed | tf_op | source)
XLA Modules:
  0.0 247.1 jit_solution(2533522667933192728)
XLA Ops:
  2.0 5.5 %collective-permute-start.7 = (bf16[256,4,128]{2,0,1:T(8,128)(2,1)S(1)}, bf16[256,4,128]{2,0,1:T(8,128)(2,1)}, u32[]{:S(2)}, u32[]{:S(2)}) collective-permute-start(bf16[256,4,128]{2,0,1:T(8,128)(2,1)S(1)} %copy.106), channel_id=1, source_target_pairs={{0,4},{4,8},{8,12},{12,16},{16,20},{20,24},{24,28},{1,5},{5,9},{9,... | collective-permute-start | bytes 786440 | tf_op jit(solution)/shard_map/ppermute | solution.py:17
  7.5 3.5 %collective-permute-start.6 = (bf16[256,4,128]{2,0,1:T(8,128)(2,1)S(1)}, bf16[256,4,128]{2,0,1:T(8,128)(2,1)}, u32[]{:S(2)}, u32[]{:S(2)}) collective-permute-start(bf16[256,4,128]{2,0,1:T(8,128)(2,1)S(1)} %copy.106), channel_id=1, source_target_pairs={{0,8},{4,12},{8,16},{12,20},{16,24},{20,28},{1,9},{5,13},{9,17},{1... | collective-permute-start | bytes 786440 | tf_op jit(solution)/shard_map/ppermute | solution.py:17
  13.3 3.6 %collective-permute-start.2 = (bf16[256,4,128]{2,0,1:T(8,128)(2,1)}, bf16[256,4,128]{2,0,1:T(8,128)(2,1)}, u32[]{:S(2)}, u32[]{:S(2)}) collective-permute-start(bf16[256,4,128]{2,0,1:T(8,128)(2,1)} %multiply_convert_fusion.1), channel_id=1, source_target_pairs={{0,8},{4,12},{8,16},{12,20},{16,24},{20,28},{1,9},{5,13},{9,17},{1... | collective-permute-start | bytes 786440 | tf_op jit(solution)/shard_map/ppermute | solution.py:17
  16.9 2.9 %collective-permute-start.1 = (bf16[256,4,128]{2,0,1:T(8,128)(2,1)}, bf16[256,4,128]{2,0,1:T(8,128)(2,1)}, u32[]{:S(2)}, u32[]{:S(2)}) collective-permute-start(bf16[256,4,128]{2,0,1:T(8,128)(2,1)} %multiply_convert_fusion.1), channel_id=1, source_target_pairs={{0,12},{4,16},{8,20},{12,24},{16,28},{1,13},{5,17},{9,21},{13,25},... | collective-permute-start | bytes 786440 | tf_op jit(solution)/shard_map/ppermute | solution.py:17
  19.8 2.0 collective-permute-start
  24.8 8.0 %collective-permute-done = bf16[256,4,128]{2,0,1:T(8,128)(2,1)} collective-permute-done((bf16[256,4,128]{2,0,1:T(8,128)(2,1)}, bf16[256,4,128]{2,0,1:T(8,128)(2,1)}, u32[]{:S(2)}, u32[]{:S(2)}) %collective-permute-start) | collective-permute-done | bytes 262176 | tf_op jit(solution)/shard_map/ppermute | solution.py:17
  32.8 5.7 %collective-permute-start.3 = (bf16[256,4,128]{2,0,1:T(8,128)(2,1)}, bf16[256,4,128]{2,0,1:T(8,128)(2,1)S(1)}, u32[]{:S(2)}, u32[]{:S(2)}) collective-permute-start(bf16[256,4,128]{2,0,1:T(8,128)(2,1)} %multiply_convert_fusion.1), channel_id=1, source_target_pairs={{0,4},{4,8},{8,12},{12,16},{16,20},{20,24},{24,28},{1,5},{5,9},{9,... | collective-permute-start | bytes 786440 | tf_op jit(solution)/shard_map/ppermute | solution.py:17
  38.5 1.7 constant_dynamic-update-slice_fusion.4
  40.2 16.8 %collective-permute-start.5 = (bf16[256,4,128]{2,0,1:T(8,128)(2,1)S(1)}, bf16[256,4,128]{2,0,1:T(8,128)(2,1)}, u32[]{:S(2)}, u32[]{:S(2)}) collective-permute-start(bf16[256,4,128]{2,0,1:T(8,128)(2,1)S(1)} %copy.106), channel_id=1, source_target_pairs={{0,12},{4,16},{8,20},{12,24},{16,28},{1,13},{5,17},{9,21},{13,25},... | collective-permute-start | bytes 786440 | tf_op jit(solution)/shard_map/ppermute | solution.py:17
  56.9 1.7 constant_dynamic-update-slice_fusion.3
  58.6 14.0 %collective-permute-start.4 = (bf16[256,4,128]{2,0,1:T(8,128)(2,1)S(1)}, bf16[256,4,128]{2,0,1:T(8,128)(2,1)}, u32[]{:S(2)}, u32[]{:S(2)}) collective-permute-start(bf16[256,4,128]{2,0,1:T(8,128)(2,1)S(1)} %copy.106), channel_id=1, source_target_pairs={{0,16},{4,20},{8,24},{12,28},{1,17},{5,21},{9,25},{13,29},{2,18},{... | collective-permute-start | bytes 786440 | tf_op jit(solution)/shard_map/ppermute | solution.py:17
  76.1 3.5 %fusion.77 = f32[2,256,1280]{1,2,0:T(8,128)} fusion(pred[256,1280]{0,1:T(8,128)(4,1)} %fusion.95, bf16[1280,4,128]{2,0,1:T(8,128)(2,1)} %constant_dynamic-update-slice_fusion, bf16[256,8,128]{2,0,1:T(8,128)(2,1)S(1)} %copy-done.7), kind=kOutput, calls=%fused_computation.86 | convolution fusion | flops 169740032 | bytes 3407872 | tf_op jit(solution)/shard_map/div | solution.py:67
  79.6 3.5 %fusion.79 = f32[2,256,1280]{1,2,0:T(8,128)} fusion(pred[256,1280]{0,1:T(8,128)(4,1)} %fusion.95, bf16[1280,4,128]{2,0,1:T(8,128)(2,1)} %constant_dynamic-update-slice_fusion, bf16[256,8,128]{2,0,1:T(8,128)(2,1)S(1)} %copy-done.7), kind=kOutput, calls=%fused_computation.88 | convolution fusion | flops 169740032 | bytes 3407872 | tf_op jit(solution)/shard_map/div | solution.py:67
  83.0 3.5 %fusion.81 = f32[2,256,1280]{1,2,0:T(8,128)} fusion(pred[256,1280]{0,1:T(8,128)(4,1)} %fusion.95, bf16[1280,4,128]{2,0,1:T(8,128)(2,1)} %constant_dynamic-update-slice_fusion, bf16[256,8,128]{2,0,1:T(8,128)(2,1)S(1)} %copy-done.7), kind=kOutput, calls=%fused_computation.90 | convolution fusion | flops 169740032 | bytes 3407872 | tf_op jit(solution)/shard_map/div | solution.py:67
  86.5 3.5 %fusion.91 = f32[2,256,1280]{1,2,0:T(8,128)} fusion(pred[256,1280]{0,1:T(8,128)(4,1)} %fusion.95, bf16[1280,4,128]{2,0,1:T(8,128)(2,1)} %constant_dynamic-update-slice_fusion, bf16[256,8,128]{2,0,1:T(8,128)(2,1)S(1)} %copy-done.7), kind=kOutput, calls=%fused_computation.100 | convolution fusion | flops 169740032 | bytes 3407872 | tf_op jit(solution)/shard_map/div | solution.py:67
  95.5 2.0 convolution_bitcast_fusion
  97.5 5.8 %fusion.96 = f32[256,2,128]{2,0,1:T(8,128)} fusion(f32[2,256,1280]{1,2,0:T(8,128)} %fusion.77, f32[2,256,1280]{1,2,0:T(8,128)} %convolution_bitcast_fusion, bf16[1280,4,128]{2,0,1:T(8,128)(2,1)} %constant_dynamic-update-slice_fusion), kind=kOutput, calls=%fused_computation.106 | convolution fusion | flops 171050752 | bytes 11075584 | tf_op jit(solution)/shard_map/gtc,cd->tgd/dot_general | solution.py:73
  103.3 5.6 %fusion.48 = bf16[1280,1,128]{2,0,1:T(8,128)(2,1)} fusion(f32[2,256,1280]{1,2,0:T(8,128)} %fusion.77, f32[2,256,1280]{1,2,0:T(8,128)} %convolution_bitcast_fusion, bf16[256,8,128]{2,0,1:T(8,128)(2,1)S(1)} %copy-done.7), kind=kOutput, calls=%fused_computation.68 | convolution fusion | flops 171214592 | bytes 10944512 | tf_op jit(solution)/shard_map/gtc,tgd->cd/dot_general | solution.py:76
  108.9 3.2 %convolution_bitcast_fusion.1 = f32[2,256,1280]{1,2,0:T(8,128)} fusion(bf16[1280,4,128]{2,0,1:T(8,128)(2,1)} %copy-done.4, bf16[256,8,128]{0,2,1:T(8,128)(2,1)S(1)} %bitcast.191), kind=kOutput, calls=%fused_computation.21 | convolution fusion | flops 167772160 | bytes 3080192 | tf_op jit(solution)/shard_map/tgd,cd->gtc/dot_general | solution.py:68
  113.3 5.8 %fusion.99 = f32[256,2,128]{2,0,1:T(8,128)} fusion(f32[2,256,1280]{1,2,0:T(8,128)} %fusion.79, f32[2,256,1280]{1,2,0:T(8,128)} %convolution_bitcast_fusion.1, bf16[1280,4,128]{2,0,1:T(8,128)(2,1)} %constant_dynamic-update-slice_fusion), kind=kOutput, calls=%fused_computation.107 | convolution fusion | flops 171050752 | bytes 11075584 | tf_op jit(solution)/shard_map/gtc,cd->tgd/dot_general | solution.py:73
  119.1 5.6 %fusion.49 = bf16[1280,1,128]{2,0,1:T(8,128)(2,1)} fusion(f32[2,256,1280]{1,2,0:T(8,128)} %fusion.79, f32[2,256,1280]{1,2,0:T(8,128)} %convolution_bitcast_fusion.1, bf16[256,8,128]{2,0,1:T(8,128)(2,1)S(1)} %copy-done.7), kind=kOutput, calls=%fused_computation.69 | convolution fusion | flops 171214592 | bytes 10944512 | tf_op jit(solution)/shard_map/gtc,tgd->cd/dot_general | solution.py:76
  124.7 3.1 %convolution_bitcast_fusion.2 = f32[2,256,1280]{1,2,0:T(8,128)} fusion(bf16[1280,4,128]{2,0,1:T(8,128)(2,1)} %copy-done.4, bf16[256,8,128]{0,2,1:T(8,128)(2,1)S(1)} %bitcast.193), kind=kOutput, calls=%fused_computation.22 | convolution fusion | flops 167772160 | bytes 3080192 | tf_op jit(solution)/shard_map/tgd,cd->gtc/dot_general | solution.py:68
  129.1 5.8 %fusion.102 = f32[256,2,128]{2,0,1:T(8,128)} fusion(f32[2,256,1280]{1,2,0:T(8,128)} %fusion.81, f32[2,256,1280]{1,2,0:T(8,128)} %convolution_bitcast_fusion.2, bf16[1280,4,128]{2,0,1:T(8,128)(2,1)} %constant_dynamic-update-slice_fusion), kind=kOutput, calls=%fused_computation.108 | convolution fusion | flops 171050752 | bytes 11075584 | tf_op jit(solution)/shard_map/gtc,cd->tgd/dot_general | solution.py:73
  134.9 5.6 %fusion.50 = bf16[1280,1,128]{2,0,1:T(8,128)(2,1)} fusion(f32[2,256,1280]{1,2,0:T(8,128)} %fusion.81, f32[2,256,1280]{1,2,0:T(8,128)} %convolution_bitcast_fusion.2, bf16[256,8,128]{2,0,1:T(8,128)(2,1)S(1)} %copy-done.7), kind=kOutput, calls=%fused_computation.70 | convolution fusion | flops 171214592 | bytes 10944512 | tf_op jit(solution)/shard_map/gtc,tgd->cd/dot_general | solution.py:76
  140.5 3.1 %convolution_bitcast_fusion.3 = f32[2,256,1280]{1,2,0:T(8,128)} fusion(bf16[1280,4,128]{2,0,1:T(8,128)(2,1)} %copy-done.4, bf16[256,8,128]{0,2,1:T(8,128)(2,1)S(1)} %bitcast.195), kind=kOutput, calls=%fused_computation.23 | convolution fusion | flops 167772160 | bytes 3080192 | tf_op jit(solution)/shard_map/tgd,cd->gtc/dot_general | solution.py:68
  144.9 6.0 %fusion.105 = f32[256,2,128]{2,0,1:T(8,128)} fusion(f32[2,256,1280]{1,2,0:T(8,128)} %fusion.91, f32[2,256,1280]{1,2,0:T(8,128)} %convolution_bitcast_fusion.3, bf16[1280,4,128]{2,0,1:T(8,128)(2,1)} %constant_dynamic-update-slice_fusion), kind=kOutput, calls=%fused_computation.109 | convolution fusion | flops 171050752 | bytes 11075584 | tf_op jit(solution)/shard_map/gtc,cd->tgd/dot_general | solution.py:73
  151.0 5.6 %fusion.51 = bf16[1280,1,128]{2,0,1:T(8,128)(2,1)} fusion(f32[2,256,1280]{1,2,0:T(8,128)} %fusion.91, f32[2,256,1280]{1,2,0:T(8,128)} %convolution_bitcast_fusion.3, bf16[256,8,128]{2,0,1:T(8,128)(2,1)S(1)} %copy-done.7), kind=kOutput, calls=%fused_computation.71 | convolution fusion | flops 171214592 | bytes 10944512 | tf_op jit(solution)/shard_map/gtc,tgd->cd/dot_general | solution.py:76
  168.3 2.0 copy.154
  175.4 12.9 %collective-permute-done.15 = bf16[256,4,128]{0,2,1:T(8,128)(2,1)} collective-permute-done((bf16[256,4,128]{0,2,1:T(8,128)(2,1)}, bf16[256,4,128]{0,2,1:T(8,128)(2,1)}, u32[]{:S(2)}, u32[]{:S(2)}) %collective-permute-start.15) | collective-permute-done | bytes 262176 | tf_op jit(solution)/shard_map/ppermute | solution.py:17
  193.1 23.3 %collective-permute-done.11 = bf16[256,4,128]{2,0,1:T(8,128)(2,1)} collective-permute-done((bf16[256,4,128]{2,0,1:T(8,128)(2,1)}, bf16[256,4,128]{2,0,1:T(8,128)(2,1)}, u32[]{:S(2)}, u32[]{:S(2)}) %collective-permute-start.11) | collective-permute-done | bytes 262176 | tf_op jit(solution)/shard_map/ppermute | solution.py:17
  219.3 5.6 %all-reduce.1 = (f32[128]{0:T(128)S(1)}, f32[128]{0:T(128)S(1)}) all-reduce(f32[128]{0:T(128)S(1)} %bitcast_reduce_fusion, f32[128]{0:T(128)S(1)} %get-tuple-element.20), channel_id=1, replica_groups=mesh['ctx'=8,'tp'=4] {'tp'}, use_global_device_ids=true, to_apply=%region_14.15 | all-reduce | flops 256 | bytes 2048 | tf_op jit(solution)/shard_map/psum | solution.py:98
  225.0 21.6 %all-reduce = (f32[128]{0:T(128)S(1)}, f32[128]{0:T(128)S(1)}) all-reduce(f32[128]{0:T(128)S(1)} %get-tuple-element.24, f32[128]{0:T(128)S(1)} %get-tuple-element.25), channel_id=1, replica_groups=mesh['ctx'=8,'tp'=4] {'ctx'}, use_global_device_ids=true, to_apply=%region_15.16 | all-reduce | flops 256 | bytes 2048 | tf_op jit(solution)/shard_map/psum | solution.py:99
  (95 shorter events, 44.1 us)
Async XLA Ops:
  0.6 11.7 %copy-start.12 = (f32[128]{0:T(128)S(1)}, f32[128]{0:T(128)}, u32[]{:S(2)}) copy-start(f32[128]{0:T(128)} %param.11) | copy-start | bytes 1540
  0.6 21.1 %copy-start.5 = (bf16[256,1024]{1,0:T(8,128)(2,1)S(1)}, bf16[256,1024]{1,0:T(8,128)(2,1)}, u32[]{:S(2)}) copy-start(bf16[256,1024]{1,0:T(8,128)(2,1)} %param.6) | copy-start | bytes 1572868
  2.0 91.1 %collective-permute-start.7 = (bf16[256,4,128]{2,0,1:T(8,128)(2,1)S(1)}, bf16[256,4,128]{2,0,1:T(8,128)(2,1)}, u32[]{:S(2)}, u32[]{:S(2)}) collective-permute-start(bf16[256,4,128]{2,0,1:T(8,128)(2,1)S(1)} %copy.106), channel_id=1, source_target_pairs={{0,4},{4,8},{8,12},{12,16},{16,20},{20,24},{24,28},{1,5},{5,9},{9,... | collective-permute-start | bytes 786440 | tf_op jit(solution)/shard_map/ppermute | solution.py:17
  7.5 84.6 %collective-permute-start.6 = (bf16[256,4,128]{2,0,1:T(8,128)(2,1)S(1)}, bf16[256,4,128]{2,0,1:T(8,128)(2,1)}, u32[]{:S(2)}, u32[]{:S(2)}) collective-permute-start(bf16[256,4,128]{2,0,1:T(8,128)(2,1)S(1)} %copy.106), channel_id=1, source_target_pairs={{0,8},{4,12},{8,16},{12,20},{16,24},{20,28},{1,9},{5,13},{9,17},{1... | collective-permute-start | bytes 786440 | tf_op jit(solution)/shard_map/ppermute | solution.py:17
  12.1 11.3 %copy-start.13 = (f32[128]{0:T(128)S(1)}, f32[128]{0:T(128)}, u32[]{:S(2)}) copy-start(f32[128]{0:T(128)} %param.10) | copy-start | bytes 1540
  13.3 11.3 %copy-start.6 = (bf16[256,1024]{1,0:T(8,128)(2,1)S(1)}, bf16[256,1024]{1,0:T(8,128)(2,1)}, u32[]{:S(2)}) copy-start(bf16[256,1024]{1,0:T(8,128)(2,1)} %param.9) | copy-start | bytes 1572868
  13.3 45.4 %collective-permute-start.2 = (bf16[256,4,128]{2,0,1:T(8,128)(2,1)}, bf16[256,4,128]{2,0,1:T(8,128)(2,1)}, u32[]{:S(2)}, u32[]{:S(2)}) collective-permute-start(bf16[256,4,128]{2,0,1:T(8,128)(2,1)} %multiply_convert_fusion.1), channel_id=1, source_target_pairs={{0,8},{4,12},{8,16},{12,20},{16,24},{20,28},{1,9},{5,13},{9,17},{1... | collective-permute-start | bytes 786440 | tf_op jit(solution)/shard_map/ppermute | solution.py:17
  16.9 23.3 %collective-permute-start.1 = (bf16[256,4,128]{2,0,1:T(8,128)(2,1)}, bf16[256,4,128]{2,0,1:T(8,128)(2,1)}, u32[]{:S(2)}, u32[]{:S(2)}) collective-permute-start(bf16[256,4,128]{2,0,1:T(8,128)(2,1)} %multiply_convert_fusion.1), channel_id=1, source_target_pairs={{0,12},{4,16},{8,20},{12,24},{16,28},{1,13},{5,17},{9,21},{13,25},... | collective-permute-start | bytes 786440 | tf_op jit(solution)/shard_map/ppermute | solution.py:17
  19.8 13.0 %collective-permute-start = (bf16[256,4,128]{2,0,1:T(8,128)(2,1)}, bf16[256,4,128]{2,0,1:T(8,128)(2,1)}, u32[]{:S(2)}, u32[]{:S(2)}) collective-permute-start(bf16[256,4,128]{2,0,1:T(8,128)(2,1)} %multiply_convert_fusion.1), channel_id=1, source_target_pairs={{0,16},{4,20},{8,24},{12,28},{1,17},{5,21},{9,25},{13,29},{2,18},{... | collective-permute-start | bytes 786440 | tf_op jit(solution)/shard_map/ppermute | solution.py:17
  24.8 51.2 %copy-start.7 = (bf16[256,8,128]{2,0,1:T(8,128)(2,1)S(1)}, bf16[256,8,128]{2,0,1:T(8,128)(2,1)}, u32[]{:S(2)}) copy-start(bf16[256,8,128]{2,0,1:T(8,128)(2,1)} %multiply_convert_fusion) | copy-start | bytes 1572868
  32.8 41.6 %collective-permute-start.3 = (bf16[256,4,128]{2,0,1:T(8,128)(2,1)}, bf16[256,4,128]{2,0,1:T(8,128)(2,1)S(1)}, u32[]{:S(2)}, u32[]{:S(2)}) collective-permute-start(bf16[256,4,128]{2,0,1:T(8,128)(2,1)} %multiply_convert_fusion.1), channel_id=1, source_target_pairs={{0,4},{4,8},{8,12},{12,16},{16,20},{20,24},{24,28},{1,5},{5,9},{9,... | collective-permute-start | bytes 786440 | tf_op jit(solution)/shard_map/ppermute | solution.py:17
  40.2 51.0 %collective-permute-start.5 = (bf16[256,4,128]{2,0,1:T(8,128)(2,1)S(1)}, bf16[256,4,128]{2,0,1:T(8,128)(2,1)}, u32[]{:S(2)}, u32[]{:S(2)}) collective-permute-start(bf16[256,4,128]{2,0,1:T(8,128)(2,1)S(1)} %copy.106), channel_id=1, source_target_pairs={{0,12},{4,16},{8,20},{12,24},{16,28},{1,13},{5,17},{9,21},{13,25},... | collective-permute-start | bytes 786440 | tf_op jit(solution)/shard_map/ppermute | solution.py:17
  58.6 31.4 %collective-permute-start.4 = (bf16[256,4,128]{2,0,1:T(8,128)(2,1)S(1)}, bf16[256,4,128]{2,0,1:T(8,128)(2,1)}, u32[]{:S(2)}, u32[]{:S(2)}) collective-permute-start(bf16[256,4,128]{2,0,1:T(8,128)(2,1)S(1)} %copy.106), channel_id=1, source_target_pairs={{0,16},{4,20},{8,24},{12,28},{1,17},{5,21},{9,25},{13,29},{2,18},{... | collective-permute-start | bytes 786440 | tf_op jit(solution)/shard_map/ppermute | solution.py:17
  90.0 4.2 %copy-start.3 = (f32[2,256,1280]{1,2,0:T(8,128)S(1)}, f32[2,256,1280]{1,2,0:T(8,128)}, u32[]{:S(2)}) copy-start(f32[2,256,1280]{1,2,0:T(8,128)} %fusion.77) | copy-start | bytes 7864324
  94.2 1.3 copy-start.4
  108.9 3.2 %copy-start.2 = (f32[2,256,1280]{1,2,0:T(8,128)S(1)}, f32[2,256,1280]{1,2,0:T(8,128)}, u32[]{:S(2)}) copy-start(f32[2,256,1280]{1,2,0:T(8,128)} %fusion.79) | copy-start | bytes 7864324
  124.7 3.1 %copy-start.1 = (f32[2,256,1280]{1,2,0:T(8,128)S(1)}, f32[2,256,1280]{1,2,0:T(8,128)}, u32[]{:S(2)}) copy-start(f32[2,256,1280]{1,2,0:T(8,128)} %fusion.81) | copy-start | bytes 7864324
  140.5 3.1 %copy-start = (f32[2,256,1280]{1,2,0:T(8,128)S(1)}, f32[2,256,1280]{1,2,0:T(8,128)}, u32[]{:S(2)}) copy-start(f32[2,256,1280]{1,2,0:T(8,128)} %fusion.91) | copy-start | bytes 7864324
  156.6 7.7 %copy-start.8 = (f32[256,2,128]{2,0,1:T(8,128)S(1)}, f32[256,2,128]{2,0,1:T(8,128)}, u32[]{:S(2)}) copy-start(f32[256,2,128]{2,0,1:T(8,128)} %fusion.96) | copy-start | bytes 786436
  156.6 7.7 %copy-start.9 = (f32[256,2,128]{2,0,1:T(8,128)S(1)}, f32[256,2,128]{2,0,1:T(8,128)}, u32[]{:S(2)}) copy-start(f32[256,2,128]{2,0,1:T(8,128)} %fusion.99) | copy-start | bytes 786436
  156.6 7.7 %copy-start.10 = (f32[256,2,128]{2,0,1:T(8,128)S(1)}, f32[256,2,128]{2,0,1:T(8,128)}, u32[]{:S(2)}) copy-start(f32[256,2,128]{2,0,1:T(8,128)} %fusion.102) | copy-start | bytes 786436
  156.6 7.7 %copy-start.11 = (f32[256,2,128]{2,0,1:T(8,128)S(1)}, f32[256,2,128]{2,0,1:T(8,128)}, u32[]{:S(2)}) copy-start(f32[256,2,128]{2,0,1:T(8,128)} %fusion.105) | copy-start | bytes 786436
  159.1 15.0 %collective-permute-start.12 = (bf16[256,4,128]{0,2,1:T(8,128)(2,1)}, bf16[256,4,128]{0,2,1:T(8,128)(2,1)}, u32[]{:S(2)}, u32[]{:S(2)}) collective-permute-start(bf16[256,4,128]{0,2,1:T(8,128)(2,1)} %get-tuple-element.29), channel_id=1, source_target_pairs={{4,0},{8,4},{12,8},{16,12},{20,16},{24,20},{28,24},{5,1},{9,5},{13... | collective-permute-start | bytes 786440 | tf_op jit(solution)/shard_map/ppermute | solution.py:17
  160.4 27.9 %collective-permute-start.15 = (bf16[256,4,128]{0,2,1:T(8,128)(2,1)}, bf16[256,4,128]{0,2,1:T(8,128)(2,1)}, u32[]{:S(2)}, u32[]{:S(2)}) collective-permute-start(bf16[256,4,128]{0,2,1:T(8,128)(2,1)} %get-tuple-element.30), channel_id=1, source_target_pairs={{16,0},{20,4},{24,8},{28,12},{17,1},{21,5},{25,9},{29,13},{18,2},{... | collective-permute-start | bytes 786440 | tf_op jit(solution)/shard_map/ppermute | solution.py:17
  161.7 27.9 %collective-permute-start.14 = (bf16[256,4,128]{0,2,1:T(8,128)(2,1)}, bf16[256,4,128]{0,2,1:T(8,128)(2,1)}, u32[]{:S(2)}, u32[]{:S(2)}) collective-permute-start(bf16[256,4,128]{0,2,1:T(8,128)(2,1)} %get-tuple-element.31), channel_id=1, source_target_pairs={{12,0},{16,4},{20,8},{24,12},{28,16},{13,1},{17,5},{21,9},{25,13},... | collective-permute-start | bytes 786440 | tf_op jit(solution)/shard_map/ppermute | solution.py:17
  163.0 27.9 %collective-permute-start.13 = (bf16[256,4,128]{0,2,1:T(8,128)(2,1)}, bf16[256,4,128]{0,2,1:T(8,128)(2,1)}, u32[]{:S(2)}, u32[]{:S(2)}) collective-permute-start(bf16[256,4,128]{0,2,1:T(8,128)(2,1)} %get-tuple-element.32), channel_id=1, source_target_pairs={{8,0},{12,4},{16,8},{20,12},{24,16},{28,20},{9,1},{13,5},{17,9},{2... | collective-permute-start | bytes 786440 | tf_op jit(solution)/shard_map/ppermute | solution.py:17
  172.8 20.3 %collective-permute-start.8 = (bf16[256,4,128]{2,0,1:T(8,128)(2,1)}, bf16[256,4,128]{2,0,1:T(8,128)(2,1)}, u32[]{:S(2)}, u32[]{:S(2)}) collective-permute-start(bf16[256,4,128]{2,0,1:T(8,128)(2,1)} %get-tuple-element.33), channel_id=1, source_target_pairs={{4,0},{8,4},{12,8},{16,12},{20,16},{24,20},{28,24},{5,1},{9,5},{13... | collective-permute-start | bytes 786440 | tf_op jit(solution)/shard_map/ppermute | solution.py:17
  174.1 42.2 %collective-permute-start.11 = (bf16[256,4,128]{2,0,1:T(8,128)(2,1)}, bf16[256,4,128]{2,0,1:T(8,128)(2,1)}, u32[]{:S(2)}, u32[]{:S(2)}) collective-permute-start(bf16[256,4,128]{2,0,1:T(8,128)(2,1)} %get-tuple-element.34), channel_id=1, source_target_pairs={{16,0},{20,4},{24,8},{28,12},{17,1},{21,5},{25,9},{29,13},{18,2},{... | collective-permute-start | bytes 786440 | tf_op jit(solution)/shard_map/ppermute | solution.py:17
  188.3 28.1 %collective-permute-start.10 = (bf16[256,4,128]{2,0,1:T(8,128)(2,1)}, bf16[256,4,128]{2,0,1:T(8,128)(2,1)}, u32[]{:S(2)}, u32[]{:S(2)}) collective-permute-start(bf16[256,4,128]{2,0,1:T(8,128)(2,1)} %get-tuple-element.35), channel_id=1, source_target_pairs={{12,0},{16,4},{20,8},{24,12},{28,16},{13,1},{17,5},{21,9},{25,13},... | collective-permute-start | bytes 786440 | tf_op jit(solution)/shard_map/ppermute | solution.py:17
  189.6 26.8 %collective-permute-start.9 = (bf16[256,4,128]{2,0,1:T(8,128)(2,1)}, bf16[256,4,128]{2,0,1:T(8,128)(2,1)}, u32[]{:S(2)}, u32[]{:S(2)}) collective-permute-start(bf16[256,4,128]{2,0,1:T(8,128)(2,1)} %get-tuple-element.36), channel_id=1, source_target_pairs={{8,0},{12,4},{16,8},{20,12},{24,16},{28,20},{9,1},{13,5},{17,9},{2... | collective-permute-start | bytes 786440 | tf_op jit(solution)/shard_map/ppermute | solution.py:17
